TPU v7x, 512 devices: a whole 4x4x16 slice. The times are simulated.
512 devices in a mesh: cuts: 32 (over z, y_hi), angle: 16 (over y_lo, x, core).
Axes of the slice: x: 4, y: 4 (y_hi: 2, y_lo: 2; y = y_hi * 2 + y_lo), z: 16, core: 2. Of those that a mesh axis runs over, the one named last changes fastest.
Arguments:
- density: bfloat16 [32, 576, 256], P('cuts', 'angle'), may hold values from 0.049804688 to 2
- kernel_blocks: bfloat16 [576, 256, 384], P('cuts'), may hold values from -0.015625 to 0.015625
Outputs:
- sinogram: bfloat16 [32, 576, 384], P('cuts', 'angle')
All inputs are finite; a program needn't handle non-finite values.
Results may differ from a plain program's by a relative error of at most 0.0012.
Values may be sent and summed in bfloat16 or wider, within the bound.
No kernel may reach another device: no remote copies, remote signals or barrier semaphores. Data moves between devices by JAX's collectives and lax.ppermute only.
A program may use at most 64 MiB of HBM per device.

v0:
```python
import jax
import jax.numpy as jnp
from jax import lax
from jax.sharding import PartitionSpec as P


def local(density, kernel_blocks):
    angles_dev = density.shape[1]
    offsets_dev = kernel_blocks.shape[0]
    angle_count = lax.axis_size("angle")
    offset_start = lax.axis_index("cuts") * offsets_dev
    block_steps = offset_start // angles_dev
    remainder = offset_start - block_steps * angles_dev
    gathered = lax.all_gather(density, "cuts", axis=0, tiled=True)
    full_cycle = lax.all_gather(gathered, "angle", axis=1, tiled=True)
    doubled = jnp.concatenate([full_cycle, full_cycle[:, :angles_dev]], axis=1)
    window_start = (lax.axis_index("angle") - block_steps - 1) % angle_count * angles_dev
    window = lax.dynamic_slice_in_dim(doubled, window_start, 2 * angles_dev, 1)

    def shifted_rows(offset_lag):
        return lax.dynamic_slice_in_dim(window, angles_dev - remainder - offset_lag, angles_dev, 1)

    offset_lags = jnp.arange(offsets_dev, dtype=jnp.int32)
    stacked = jax.vmap(shifted_rows)(offset_lags)
    contribution = lax.psum_scatter(
        jnp.einsum("lsvr,lrb->svb", stacked, kernel_blocks, preferred_element_type=jnp.float32),
        "cuts",
        scatter_dimension=0,
        tiled=True,
    )
    return contribution.astype(jnp.bfloat16)


def solution(mesh):
    return jax.shard_map(
        local,
        mesh=mesh,
        in_specs=(P("cuts", "angle", None), P("cuts", None, None)),
        out_specs=P("cuts", "angle", None),
        check_vma=False,
    )
```

profile of v0, /device:TPU:6, one launch (start us, length us, event | category | flops | bytes accessed | tf_op | source)
XLA Modules:
  0.0 747.7 jit_solution(466443494181665318)
XLA Ops:
  6.5 0.0 copy-start
  6.5 0.0 all-gather.2.cloned.1.call-start
  6.5 86.7 %all_gather.6 = bf16[32,36,256]{2,1,0:T(8,128)(2,1)S(1)} all-gather(bf16[1,36,256]{2,1,0:T(8,128)(2,1)} %param.2), channel_id=1, replica_groups=mesh['cuts'=32,'angle'=16] {'cuts'}, dimensions={0}, use_global_device_ids=true | all-gather | bytes 608256 | tf_op jit(solution)/shard_map/all_gather | solution.py:14
  93.3 0.9 copy.5
  94.2 0.0 all-gather.2.cloned.1.call-update
  94.2 0.0 reduce-scatter.4.cloned.1.call-start
  94.3 57.7 %all-gather.2.cloned.1.call-done = bf16[32,576,256]{2,0,1:T(8,128)(2,1)} async-done(((bf16[32,36,256]{2,0,1:T(8,128)(2,1)}), bf16[32,576,256]{2,0,1:T(8,128)(2,1)}) %all-gather.2.cloned.1.call-update) | async-done | bytes 9437200 | tf_op jit(solution)/shard_map/all_gather | solution.py:15
  152.1 1.1 slice.7
  153.2 2.7 fusion.2
  155.9 7.0 gather_fusion
  162.9 0.0 copy-done
  162.9 8.4 %fusion = f32[32,36,384,1]{2,0,1,3:T(8,128)S(1)} fusion(bf16[18,32,36,256]{3,1,2,0:T(8,128)(2,1)} %gather_fusion, bf16[18,256,384]{2,1,0:T(8,128)(2,1)S(1)} %copy-done), kind=kOutput, calls=%fused_computation.3 | convolution fusion | flops 4076863488 | bytes 15925248 | tf_op jit(solution)/shard_map/lsvr,lrb->svb/dot_general | solution.py:26
  171.3 2.3 copy.11
  173.6 0.0 reduce-scatter.4.cloned.1.call-update
  173.6 565.8 %reduce-scatter.4.cloned.1.call-done = f32[1,36,384]{2,1,0:T(8,128)} async-done(((f32[32,36,384]{2,1,0:T(8,128)}), f32[1,36,384]{2,1,0:T(8,128)}) %reduce-scatter.4.cloned.1.call-update) | async-done | bytes 55312
  739.5 1.4 convert_element_type.3
  (1 shorter events, 0.0 us)
Async XLA Ops:
  6.5 156.4 %copy-start = (bf16[18,256,384]{2,1,0:T(8,128)(2,1)S(1)}, bf16[18,256,384]{2,1,0:T(8,128)(2,1)}, u32[]{:S(2)}) copy-start(bf16[18,256,384]{2,1,0:T(8,128)(2,1)} %param.3) | copy-start | bytes 10616836
  6.5 145.5 %all-gather.2.cloned.1.call-start = ((), (), s32[]{:S(2)}) async-start(), calls=%async_computation.1 | async-start | bytes 10027008 | tf_op jit(solution)/shard_map/all_gather | solution.py:15
  94.2 645.2 %reduce-scatter.4.cloned.1.call-start = ((), (), s32[]{:S(2)}) async-start(), calls=%async_computation.2 | async-start | bytes 2027520
Sparse Core Ops, SparseCore 0:
  94.3 57.6 all-gather.1
  173.7 565.6 reduce-scatter.3
where the time goes:
time: 748 us
  waiting for transfers between devices  624 us (83%)
  blocking collectives  86.7 us (12%)
  between operations  13.5 us (2%)
  local copies, waits for them, and re-layouts  11.4 us (2%)
  matrix products  8.36 us (1%)
    unnamed x3, waiting for transfers between devices  566 us
    all_gather x1, blocking collectives, local(): gathered = lax.all_gather(density, 'cuts', axis=0, tiled=True)  86.7 us
    all_gather x1, waiting for transfers between devices, local(): full_cycle = lax.all_gather(gathered, 'angle', axis=1, tiled=True)  57.7 us
  transfers between devices with their start and end apart: 2, of which 2 were waited for; matrix products, arithmetic and copies ran while one was open for 0% of the time, Pallas kernels for 0%

commit v1 on v0

--- a/solution.py
+++ b/solution.py
@@ -11,7 +11,9 @@
     offset_start = lax.axis_index("cuts") * offsets_dev
     block_steps = offset_start // angles_dev
     remainder = offset_start - block_steps * angles_dev
-    gathered = lax.all_gather(density, "cuts", axis=0, tiled=True)
+    gathered = jnp.concatenate(
+        lax.all_to_all(jnp.stack([density] * lax.axis_size("cuts")), "cuts", 0, 0), axis=0
+    )
     full_cycle = lax.all_gather(gathered, "angle", axis=1, tiled=True)
     doubled = jnp.concatenate([full_cycle, full_cycle[:, :angles_dev]], axis=1)
     window_start = (lax.axis_index("angle") - block_steps - 1) % angle_count * angles_dev

time: 748 us -> 717 us (0.959)
  blocking collectives: 86.7 us -> 56.3 us
    all_gather x1 -> x0, blocking collectives: 86.7 us -> none  [local(): gathered = lax.all_gather(density, 'cuts', axis=0, tiled=True)]
    all_to_all x0 -> x1, blocking collectives: none -> 56.3 us  [local(): lax.all_to_all(jnp.stack([density] * lax.axis_size('cuts')), 'cuts', 0, 0)]
where the time goes in v1:
time: 717 us
  waiting for transfers between devices  622 us (87%)
  blocking collectives  56.3 us (8%)
  between operations  13.5 us (2%)
  local copies, waits for them, and re-layouts  12.3 us (2%)
  matrix products  8.36 us (1%)
    unnamed x3, waiting for transfers between devices  566 us
    all_to_all x1, blocking collectives, local(): lax.all_to_all(jnp.stack([density] * lax.axis_size('cuts')), 'cuts', 0, 0)  56.3 us
    all_gather x1, waiting for transfers between devices, local(): full_cycle = lax.all_gather(gathered, 'angle', axis=1, tiled=True)  56.2 us
  transfers between devices with their start and end apart: 2, of which 2 were waited for; matrix products, arithmetic and copies ran while one was open for 0% of the time, Pallas kernels for 0%

profile of v1, /device:TPU:6, one launch (start us, length us, event | category | flops | bytes accessed | tf_op | source)
XLA Modules:
  0.0 716.8 jit_solution(5891110818376929066)
XLA Ops:
  6.5 0.0 copy-start
  6.5 0.0 all-gather.3.cloned.1.call-start
  6.5 0.9 stack.2
  7.5 56.3 %all_to_all.5 = bf16[32,1,36,256]{3,2,1,0:T(8,128)(2,1)S(1)} all-to-all(bf16[32,1,36,256]{3,2,1,0:T(8,128)(2,1)S(1)} %stack.2), channel_id=1, replica_groups=mesh['cuts'=32,'angle'=16] {'cuts'}, dimensions={0} | all-to-all | bytes 1179648 | tf_op jit(solution)/shard_map/all_to_all | solution.py:15
  63.8 0.9 copy.4
  64.7 0.0 all-gather.3.cloned.1.call-update
  64.7 0.0 reduce-scatter.4.cloned.1.call-start
  64.8 56.2 %all-gather.3.cloned.1.call-done = bf16[32,1,576,256]{3,0,1,2:T(8,128)(2,1)} async-done(((bf16[32,1,36,256]{3,0,1,2:T(8,128)(2,1)}), bf16[32,1,576,256]{3,0,1,2:T(8,128)(2,1)}) %all-gather.3.cloned.1.call-update) | async-done | bytes 9437200 | tf_op jit(solution)/shard_map/all_gather | solution.py:17
  121.1 1.1 slice.7
  122.2 2.7 fusion.2
  124.9 7.0 gather_fusion
  131.9 0.0 copy-done
  131.9 8.4 %fusion = f32[32,36,384,1]{2,0,1,3:T(8,128)S(1)} fusion(bf16[18,32,36,256]{3,1,2,0:T(8,128)(2,1)} %gather_fusion, bf16[18,256,384]{2,1,0:T(8,128)(2,1)S(1)} %copy-done), kind=kOutput, calls=%fused_computation.3 | convolution fusion | flops 4076863488 | bytes 15925248 | tf_op jit(solution)/shard_map/lsvr,lrb->svb/dot_general | solution.py:28
  140.3 2.3 copy.10
  142.6 0.0 reduce-scatter.4.cloned.1.call-update
  142.6 565.9 %reduce-scatter.4.cloned.1.call-done = f32[1,36,384]{2,1,0:T(8,128)} async-done(((f32[32,36,384]{2,1,0:T(8,128)}), f32[1,36,384]{2,1,0:T(8,128)}) %reduce-scatter.4.cloned.1.call-update) | async-done | bytes 55312
  708.6 1.4 convert_element_type.3
  (1 shorter events, 0.0 us)
Async XLA Ops:
  6.5 125.4 %copy-start = (bf16[18,256,384]{2,1,0:T(8,128)(2,1)S(1)}, bf16[18,256,384]{2,1,0:T(8,128)(2,1)}, u32[]{:S(2)}) copy-start(bf16[18,256,384]{2,1,0:T(8,128)(2,1)} %param.3) | copy-start | bytes 10616836
  6.5 114.5 %all-gather.3.cloned.1.call-start = ((), (), s32[]{:S(2)}) async-start(), calls=%async_computation.2 | async-start | bytes 10027008 | tf_op jit(solution)/shard_map/all_gather | solution.py:17
  64.7 643.8 %reduce-scatter.4.cloned.1.call-start = ((), (), s32[]{:S(2)}) async-start(), calls=%async_computation.3 | async-start | bytes 2027520
Sparse Core Ops, SparseCore 0:
  64.8 56.1 all-gather.2
  142.7 565.7 reduce-scatter.3
